TPU v7x, 256 devices: a whole 4x4x8 slice. The times are simulated.
256 devices in a mesh: energy: 128 (over z, y, x), mom: 2 (over core).
Axes of the slice: x: 4, y: 4, z: 8, core: 2. Of those that a mesh axis runs over, the one named last changes fastest.
Arguments:
- lesser: bfloat16 [2, 2, 512, 65536], P('mom', None, 'energy'), may hold values from -6 to 6
- greater: bfloat16 [2, 2, 512, 65536], P('mom', None, 'energy'), may hold values from -6 to 6
- coulomb: bfloat16 [2, 4, 128, 128], P('mom'), may hold values from -0.375 to 0.375
- tile_block: int32 [4], replicated, may hold values from 0 to 3, each once
- shift_table: int32 [2, 2], replicated, may hold values from 0 to 1, each once within a row
Outputs:
- polarization: bfloat16 [2, 2, 512, 65536], P('mom', None, 'energy')
- screened: float32 [2, 2, 128, 65536], P('mom', None, 'energy')
Inputs may be any that keep to these rules, and one draw needn't show every extreme that they name: `tile_block`: each of the 4 tiles holds a different block of the pattern. `shift_table`: each row names every momentum once.
All inputs are finite; a program needn't handle non-finite values.
Results may differ from a plain program's by a relative error of at most 0.0013.
Values may be sent and summed in bfloat16 or wider, within the bound.
A program may use at most 128 MiB of HBM per device.

v0:
```python
import math

import jax
import jax.numpy as jnp
from jax import lax
from jax.sharding import PartitionSpec as P

E = 512


def rotation(product, period, sign):
    angle = 2.0 * math.pi / period * (product % period).astype(jnp.float32)
    return (jnp.cos(angle), sign * jnp.sin(angle))


def complex_einsum(form, table_re, table_im, data_re, data_im, data_axis):
    upper = jnp.concatenate((table_re, -table_im), axis=1)
    lower = jnp.concatenate((table_im, table_re), axis=1)
    table = jnp.concatenate((upper, lower), axis=0)
    data = jnp.concatenate((data_re, data_im), axis=data_axis)
    result = jnp.einsum(
        form, table, data, precision=lax.Precision.HIGH, preferred_element_type=jnp.float32
    )
    half = table_re.shape[0]
    return (result[:half], result[half:])


def transform(data_re, data_im, length, sign):
    radix = 32
    rows, width = data_re.shape
    outer = length // radix
    inner = rows // radix
    shaped_re = data_re.reshape(inner, radix, width)
    shaped_im = data_im.reshape(inner, radix, width)
    freq = jnp.arange(outer, dtype=jnp.int32)
    first_re, first_im = rotation(
        freq[:, None] * jnp.arange(inner, dtype=jnp.int32)[None, :], outer, sign
    )
    mid_re, mid_im = complex_einsum("kn,nmc->kmc", first_re, first_im, shaped_re, shaped_im, 0)
    twist_re, twist_im = rotation(
        freq[:, None] * jnp.arange(radix, dtype=jnp.int32)[None, :], length, sign
    )
    turned_re = mid_re * twist_re[:, :, None] - mid_im * twist_im[:, :, None]
    turned_im = mid_re * twist_im[:, :, None] + mid_im * twist_re[:, :, None]
    digits = jnp.arange(radix, dtype=jnp.int32)
    last_re, last_im = rotation(digits[:, None] * digits[None, :], radix, sign)
    out_re, out_im = complex_einsum("jm,kmc->jkc", last_re, last_im, turned_re, turned_im, 1)
    return (out_re.reshape(length, width), out_im.reshape(length, width))


def spectrum(pair, energies):
    return transform(pair[0].astype(jnp.float32), pair[1].astype(jnp.float32), 2 * energies, -1.0)


def correlate(left, right, rows, energies):
    count = left.shape[0]
    spec_left = [spectrum(left[k], energies) for k in range(count)]
    spec_right = [spectrum(right[k], energies) for k in range(count)]
    right_re = jnp.stack([item[0] for item in spec_right])
    right_im = jnp.stack([item[1] for item in spec_right])
    scale = 1.0 / (math.sqrt(count * energies) * 2 * energies)
    total_re = jnp.zeros_like(spec_left[0][0])
    total_im = jnp.zeros_like(spec_left[0][0])
    for k in range(count):
        other_re = lax.dynamic_index_in_dim(right_re, rows[0, k], 0, keepdims=False)
        other_im = lax.dynamic_index_in_dim(right_im, rows[0, k], 0, keepdims=False)
        total_re = total_re + spec_left[k][0] * other_re + spec_left[k][1] * other_im
        total_im = total_im + spec_left[k][1] * other_re - spec_left[k][0] * other_im
    back_re, back_im = transform(total_re, total_im, 2 * energies, 1.0)
    results = [jnp.stack([-back_im[:energies], back_re[:energies]]) * scale]
    return jnp.stack(results)


def polar_all(left, right, rows, energies):
    columns = left.shape[3]
    width = math.gcd(columns, 128)
    count_q = rows.shape[0]

    def step(index, result):
        start = index * width
        part_left = lax.dynamic_slice_in_dim(left, start, width, 3)
        part_right = lax.dynamic_slice_in_dim(right, start, width, 3)
        block = correlate(part_left, part_right, rows, energies).astype(jnp.bfloat16)
        return lax.dynamic_update_slice_in_dim(result, block, start, 3)

    empty = jnp.zeros((count_q, 2, energies, columns), jnp.bfloat16)
    return lax.fori_loop(0, columns // width, step, empty)


def screen(near, coulomb, tile_block):
    tiles_n = coulomb.shape[1]
    block = coulomb.shape[2]
    band = (tiles_n + 2) // 3
    levels = near.shape[2]
    tiles = near[0].reshape(2, levels, tiles_n, block, block)
    labels = jnp.arange(tiles_n, dtype=jnp.int32)
    onehot = tile_block[:, None] == labels[None, :]
    inverse = jnp.sum(jnp.where(onehot, labels[:, None], 0), axis=0)
    ordered = jnp.take(tiles, inverse, axis=2)
    results = []
    for r in range(band):
        for c in range(max(0, r - 1), min(band, r + 2)):
            acc = jnp.zeros((2, levels, block, block), jnp.float32)
            for l in range(max(0, r - 1), min(band, r + 2)):
                acc = acc + jnp.einsum(
                    "ij,sejk->seik",
                    coulomb[0, 2 * r + l],
                    ordered[:, :, 2 * l + c],
                    preferred_element_type=jnp.float32,
                )
            results.append(acc)
    return jnp.stack(results, axis=2).reshape(1, 2, levels, tiles_n * block * block)


def shards(lesser, greater, coulomb, tile_block, shift_table):
    left, right = (
        lax.all_to_all(lesser, "energy", split_axis=3, concat_axis=2, tiled=True),
        lax.all_to_all(greater, "energy", split_axis=3, concat_axis=2, tiled=True),
    )
    left_all, right_all = (
        lax.all_gather(left, "mom", axis=0, tiled=True),
        lax.all_gather(right, "mom", axis=0, tiled=True),
    )
    rows = lax.dynamic_slice_in_dim(shift_table, lax.axis_index("mom"), 1, 0)
    polar_cols = polar_all(left_all, right_all, rows, E)
    polarization = lax.all_to_all(polar_cols, "energy", split_axis=2, concat_axis=3, tiled=True)
    near = lax.all_to_all(
        polar_cols[:, :, : E // 4], "energy", split_axis=2, concat_axis=3, tiled=True
    )
    return (polarization, screen(near, coulomb, tile_block))


def solution(mesh):
    return jax.shard_map(
        shards,
        mesh=mesh,
        in_specs=(
            P("mom", None, "energy", None),
            P("mom", None, "energy", None),
            P("mom", None, None, None),
            P(),
            P(),
        ),
        out_specs=(P("mom", None, "energy", None), P("mom", None, "energy", None)),
        check_vma=False,
    )
```

profile of v0, /device:TPU:1, one launch (start us, length us, event | category | flops | bytes accessed | tf_op | source)
XLA Modules:
  0.0 768.4 jit_solution(1303767852040457556)
XLA Ops:
  7.2 58.7 %copy.125 = bf16[1,2,4,65536]{2,1,0,3:T(2,128)(2,1)} copy(bf16[1,2,4,65536]{3,2,1,0:T(4,128)(2,1)} %param.7) | data formatting | bytes 2097152 | tf_op args[0]
  65.9 61.1 %reshape.429 = bf16[128,2,2048]{2,1,0:T(2,128)(2,1)S(1)} reshape(bf16[65536,1,2,4]{3,2,1,0:T(2,128)(2,1)} %bitcast.190) | data formatting | bytes 2097152
  127.1 44.7 %all_to_all.63 = bf16[128,2,2048]{2,1,0:T(2,128)(2,1)S(1)} all-to-all(bf16[128,2,2048]{2,1,0:T(2,128)(2,1)S(1)} %reshape.429), channel_id=1, replica_groups=mesh['energy'=128,'mom'=2] {'energy'}, dimensions={0} | all-to-all | bytes 2097152 | tf_op jit(solution)/shard_map/all_to_all | solution.py:117
  171.8 73.1 %reshape.430 = bf16[65536,1,2,4]{3,2,1,0:T(2,128)(2,1)} reshape(bf16[128,2,2048]{2,1,0:T(2,128)(2,1)S(1)} %all_to_all.63) | data formatting | bytes 2097152
  244.9 65.3 %copy.126 = bf16[1,2,128,4,512]{4,3,2,1,0:T(4,128)(2,1)S(1)} copy(bf16[1,2,128,4,512]{3,1,4,2,0:T(2,128)(2,1)} %bitcast.188) | data formatting | bytes 2097152 | tf_op jit(solution)/shard_map/all_to_all | solution.py:117
  311.5 50.9 %copy.127 = bf16[1,2,4,65536]{2,1,0,3:T(2,128)(2,1)} copy(bf16[1,2,4,65536]{3,2,1,0:T(4,128)(2,1)S(1)} %copy-done.2) | data formatting | bytes 2097152 | tf_op args[1]
  362.4 61.1 %reshape.431 = bf16[128,2,2048]{2,1,0:T(2,128)(2,1)S(1)} reshape(bf16[65536,1,2,4]{3,2,1,0:T(2,128)(2,1)} %bitcast.191) | data formatting | bytes 2097152
  423.5 35.7 %all_to_all.64 = bf16[128,2,2048]{2,1,0:T(2,128)(2,1)S(1)} all-to-all(bf16[128,2,2048]{2,1,0:T(2,128)(2,1)S(1)} %reshape.431), channel_id=1, replica_groups=mesh['energy'=128,'mom'=2] {'energy'}, dimensions={0} | all-to-all | bytes 2097152 | tf_op jit(solution)/shard_map/all_to_all | solution.py:118
  459.2 73.1 %reshape.432 = bf16[65536,1,2,4]{3,2,1,0:T(2,128)(2,1)} reshape(bf16[128,2,2048]{2,1,0:T(2,128)(2,1)S(1)} %all_to_all.64) | data formatting | bytes 2097152
  532.3 65.3 %copy.128 = bf16[1,2,128,4,512]{4,3,2,1,0:T(4,128)(2,1)S(1)} copy(bf16[1,2,128,4,512]{3,1,4,2,0:T(2,128)(2,1)} %bitcast.189) | data formatting | bytes 2097152 | tf_op jit(solution)/shard_map/all_to_all | solution.py:118
  603.2 9.3 %all-gather.5.cloned.1.call-done = bf16[2,2,512,512]{3,2,1,0:T(8,128)(2,1)} async-done(((bf16[1,2,512,512]{3,2,1,0:T(8,128)(2,1)}), bf16[2,2,512,512]{3,2,1,0:T(8,128)(2,1)}) %all-gather.5.cloned.1.call-update) | async-done | bytes 2097168 | tf_op jit(solution)/shard_map/all_gather | solution.py:122
  614.1 82.8 %while.16 = (s32[]{:T(128)}, bf16[1,2,512,512]{3,1,0,2:T(2,128)(2,1)}, bf16[2,2,512,512]{3,2,1,0:T(8,128)(2,1)}, bf16[2,2,512,512]{3,2,1,0:T(8,128)(2,1)}, s32[]...) while((s32[]{:T(128)}, bf16[1,2,512,512]{3,1,0,2:T(2,128)(2,1)}, ...), condition=%wide.region_1.2_spmd, body=%wide.region_0.1_spmd.sunk | while | flops 815953408 | bytes 64403652 | solution.py:87
  618.7 1.5 fusion.159
  620.6 2.0 multiply_subtract_fusion.8
  639.4 1.5 fusion.159
  641.3 2.0 multiply_subtract_fusion.8
  662.0 2.0 multiply_subtract_fusion.8
  682.7 2.0 multiply_subtract_fusion.8
  696.8 1.8 slice.403
  698.7 13.6 %all-to-all-start.3 = ((bf16[1,2,128,512]{3,1,0,2:T(2,128)(2,1)}), bf16[1,2,128,512]{3,1,0,2:T(2,128)(2,1)S(1)}, u32[]{:S(2)}, u32[]{:S(2)}) async-start(bf16[1,2,128,512]{3,1,0,2:T(2,128)(2,1)} %slice.403), calls=%async_computation.3 | async-start | bytes 524288 | tf_op jit(solution)/shard_map/all_to_all | solution.py:127
  712.3 13.8 %all-to-all-done.3 = bf16[1,2,128,512]{3,1,0,2:T(2,128)(2,1)S(1)} async-done(((bf16[1,2,128,512]{3,1,0,2:T(2,128)(2,1)}), bf16[1,2,128,512]{3,1,0,2:T(2,128)(2,1)S(1)}, u32[]{:S(2)}, u32[]{:S(2)}) %all-to-all-start.3) | async-done | bytes 262176 | tf_op jit(solution)/shard_map/all_to_all | solution.py:127
  726.2 6.2 all-to-all-start.2
  735.9 23.8 %all-to-all-done.2 = bf16[1,2,512,512]{3,1,0,2:T(2,128)(2,1)S(1)} async-done(((bf16[1,2,512,512]{3,1,0,2:T(2,128)(2,1)}), bf16[1,2,512,512]{3,1,0,2:T(2,128)(2,1)S(1)}, u32[]{:S(2)}, u32[]{:S(2)}) %all-to-all-start.2) | async-done | bytes 1048608 | tf_op jit(solution)/shard_map/all_to_all | solution.py:126
  760.0 1.6 all_to_all.57
  (242 shorter events, 78.7 us)
Async XLA Ops:
  7.2 591.6 %copy-start = (s32[2,2]{1,0:T(2,128)S(1)}, s32[2,2]{1,0:T(2,128)}, u32[]{:S(2)}) copy-start(s32[2,2]{1,0:T(2,128)} %param.11) | copy-start | bytes 52
  7.2 596.0 %all-gather.3.cloned.1.call-start = ((), (), s32[]{:S(2)}) async-start(), calls=%async_computation.4 | async-start | bytes 3145728 | tf_op jit(solution)/shard_map/all_gather | solution.py:121
  171.8 139.6 %copy-start.2 = (bf16[1,2,4,65536]{3,2,1,0:T(4,128)(2,1)S(1)}, bf16[1,2,4,65536]{3,2,1,0:T(4,128)(2,1)}, u32[]{:S(2)}) copy-start(bf16[1,2,4,65536]{3,2,1,0:T(4,128)(2,1)} %param.8) | copy-start | bytes 3145732
  311.4 301.1 %all-gather.5.cloned.1.call-start = ((), (), s32[]{:S(2)}) async-start(), calls=%async_computation.5 | async-start | bytes 3145728 | tf_op jit(solution)/shard_map/all_gather | solution.py:122
  614.0 98.2 %copy-start.4 = (s32[4]{0:T(128)S(1)}, s32[4]{0:T(128)}, u32[]{:S(2)}) copy-start(s32[4]{0:T(128)} %param.10) | copy-start | bytes 52
  614.0 119.4 %copy-start.3 = (bf16[1,4,128,128]{3,2,1,0:T(8,128)(2,1)S(1)}, bf16[1,4,128,128]{3,2,1,0:T(8,128)(2,1)}, u32[]{:S(2)}) copy-start(bf16[1,4,128,128]{3,2,1,0:T(8,128)(2,1)} %param.9) | copy-start | bytes 393220
  696.8 64.8 %copy-start.1 = (s32[2,2]{1,0:T(2,128)S(1)}, s32[2,2]{1,0:T(2,128)}, u32[]{:S(2)}) copy-start(s32[2,2]{1,0:T(2,128)} %param.11) | copy-start | bytes 52
  698.7 27.5 %all-to-all-start.3 = ((bf16[1,2,128,512]{3,1,0,2:T(2,128)(2,1)}), bf16[1,2,128,512]{3,1,0,2:T(2,128)(2,1)S(1)}, u32[]{:S(2)}, u32[]{:S(2)}) async-start(bf16[1,2,128,512]{3,1,0,2:T(2,128)(2,1)} %slice.403), calls=%async_computation.3 | async-start | bytes 524288 | tf_op jit(solution)/shard_map/all_to_all | solution.py:127
  726.2 33.5 %all-to-all-start.2 = ((bf16[1,2,512,512]{3,1,0,2:T(2,128)(2,1)}), bf16[1,2,512,512]{3,1,0,2:T(2,128)(2,1)S(1)}, u32[]{:S(2)}, u32[]{:S(2)}) async-start(bf16[1,2,512,512]{3,1,0,2:T(2,128)(2,1)} %get-tuple-element.179), calls=%async_computation.2 | async-start | bytes 2097152 | tf_op jit(solution)/shard_map/all_to_all | solution.py:126
Sparse Core Ops, SparseCore 0:
  311.5 12.8 all-gather.2
  598.9 13.5 all-gather.4
where the time goes:
time: 779 us; the launch traced here: 768 us
  local copies, waits for them, and re-layouts  541 us (69%)
  blocking collectives  80.4 us (10%)
  waiting for transfers between devices  47 us (6%)
  matrix products  39.7 us (5%)
  other arithmetic  21.5 us (3%)
  starting transfers between devices  19.8 us (3%)
  between operations  18 us (2%)
    unnamed x16, local copies, waits for them, and re-layouts  378 us
    all_to_all x2, local copies, waits for them, and re-layouts, shards(): lax.all_to_all(greater, 'energy', split_axis=3, concat_axis=2, tiled=True)  66.5 us
    all_to_all x2, local copies, waits for them, and re-layouts, shards(): lax.all_to_all(lesser, 'energy', split_axis=3, concat_axis=2, tiled=True)  66.4 us
    all_to_all x1, blocking collectives, shards(): lax.all_to_all(lesser, 'energy', split_axis=3, concat_axis=2, tiled=True)  44.7 us
    dot_general x40, matrix products, complex_einsum(): jnp.einsum(form, table, data, precision=lax.Precision.HIGH, preferred_ele...  38.4 us
    all_to_all x1, blocking collectives, shards(): lax.all_to_all(greater, 'energy', split_axis=3, concat_axis=2, tiled=True)  35.7 us
    all_to_all x1, waiting for transfers between devices, shards(): lax.all_to_all(polar_cols, 'energy', split_axis=2, concat_axis=3, tiled=T...  23.8 us
  transfers between devices with their start and end apart: 4, of which 3 were waited for; matrix products, arithmetic and copies ran while one was open for 33% of the time, Pallas kernels for 0%

commit v1 on v0

v1 whole, which is shorter than its diff:
```python
import math

import jax
import jax.numpy as jnp
import numpy as np
from jax import lax
from jax.experimental import pallas as pl
from jax.experimental.pallas import tpu as pltpu
from jax.sharding import PartitionSpec as P

E = 512
L = 128
FREQ = 2 * L
BLOCKS = E // L
CHIPS = 128
NNZ = 65536
PART = 128
MESH = pl.DeviceIdType.MESH


def split(table):
    high = table.astype(jnp.bfloat16)
    low = (table - high.astype(np.float64)).astype(jnp.bfloat16)
    return np.stack([high, low])


def tables():
    freq = np.concatenate([np.arange(0, FREQ, 2), np.arange(1, FREQ, 2)])
    angle = 2.0 * np.pi / FREQ * ((freq[:, None] * np.arange(L)[None, :]) % FREQ)
    cos, sin = np.cos(angle), np.sin(angle)
    forward = np.block([[cos, sin], [-sin, cos]])
    scale = 1.0 / (math.sqrt(2 * E) * FREQ)
    inverse = np.block([[-sin.T, -cos.T], [cos.T, -sin.T]]) * scale
    return split(forward), split(inverse)


def dot(a, b):
    return jnp.dot(a, b, preferred_element_type=jnp.float32)


def forward(got, b, tf, spec):
    @pl.loop(0, 8)
    def _(step):
        g, k, pair = step // 4, (step // 2) % 2, step % 2
        halves = []
        for h in range(2):
            rows = pl.ds((pair * 2 + h) * 32, 32)
            parts = [got[b, g, s, k, rows].reshape(L, PART) for s in range(2)]
            halves.append(jnp.concatenate(parts, axis=0))
        data = jnp.concatenate(halves, axis=1)
        result = dot(tf[0], data) + dot(tf[1], data)
        for h in range(2):
            for part in range(2):
                spec[g, k, pair * 2 + h, part] = result[
                    part * FREQ : (part + 1) * FREQ, h * PART : (h + 1) * PART
                ]


def products(shift, spec, mix):
    for q in range(2):
        for odd in range(2):

            @pl.loop(0, L // 16)
            def _(tile):
                rows = pl.ds(pl.multiple_of(odd * L + tile * 16, 16), 16)
                total = [[None, None] for _ in range(BLOCKS)]

                def add(d, part, value):
                    old = total[d][part]
                    total[d][part] = value if old is None else old + value

                for k in range(2):
                    other = shift[q, k]
                    left = [[spec[0, k, a, part, rows] for part in range(2)] for a in range(BLOCKS)]
                    for c in range(BLOCKS):
                        right_re = spec[1, other, c, 0, rows]
                        right_im = spec[1, other, c, 1, rows]
                        for d in range(BLOCKS - c):
                            re, im = left[c + d]
                            add(d, 0, re * right_re + im * right_im)
                            add(d, 1, im * right_re - re * right_im)
                for d in range(BLOCKS):
                    for part in range(2):
                        value = total[d][part]
                        if d + 1 < BLOCKS:
                            nxt = total[d + 1][part]
                            value = value - nxt if odd else value + nxt
                        high = value.astype(jnp.bfloat16)
                        low = (value - high.astype(jnp.float32)).astype(jnp.bfloat16)
                        mix[0, q, d, part, rows] = high
                        mix[1, q, d, part, rows] = low


def backward(b, ti, mix, swap, polar, near):
    for q in range(2):
        for pair in range(2):
            datas = []
            for level in range(2):
                halves = [mix[level, q, pair * 2 + h].reshape(2 * FREQ, PART) for h in range(2)]
                datas.append(jnp.concatenate(halves, axis=1))
            result = dot(ti[0], datas[0]) + dot(ti[0], datas[1]) + dot(ti[1], datas[0])
            result = result.astype(jnp.bfloat16)
            for h in range(2):
                for s in range(2):
                    value = result[s * L : (s + 1) * L, h * PART : (h + 1) * PART]
                    polar[b, q, s, pl.ds((pair * 2 + h) * 32, 32)] = value.reshape(32, 4, PART)
            if pair == 0:
                value = dot(swap[...], result[:, :PART]).astype(jnp.bfloat16)
                near[q, :, b] = value.reshape(L, 2, PART)


def screening(tile_block, weights, got, out):
    place = []
    for label in range(4):
        where = jnp.int32(0)
        for t in range(1, 4):
            where = jnp.where(tile_block[t] == label, t, where)
        place.append(where)
    sides = []
    for l in range(2):
        tiles = [got[place[2 * l + c]].reshape(2 * L, PART) for c in range(2)]
        sides.append(jnp.concatenate(tiles, axis=1))
    data = jnp.concatenate(sides, axis=0)
    for r in range(2):
        result = dot(weights[r], data)
        for c in range(2):
            for s in range(2):
                out[s, 2 * r + c] = result[s * L : (s + 1) * L, c * PART : (c + 1) * PART]


def prepare(coulomb, weights, swap):
    row = lax.broadcasted_iota(jnp.int32, (2 * L, 2 * L), 0)
    col = lax.broadcasted_iota(jnp.int32, (2 * L, 2 * L), 1)
    swap[...] = jnp.where(col == (row % 2) * L + row // 2, 1.0, 0.0).astype(jnp.bfloat16)
    wide_row = lax.broadcasted_iota(jnp.int32, (L, 2 * L), 0)
    wide_col = lax.broadcasted_iota(jnp.int32, (L, 2 * L), 1)
    for s in range(2):
        spread = jnp.where(wide_col == 2 * wide_row + s, 1.0, 0.0).astype(jnp.bfloat16)
        for r in range(2):
            for l in range(2):
                weights[r, s * L : (s + 1) * L, l * 2 * L : (l + 1) * 2 * L] = dot(
                    coulomb[0, 2 * r + l], spread
                ).astype(jnp.bfloat16)


def zigzag(i, n):
    return (i % 2) * ((i + 1) // 2) + (1 - i % 2) * ((n - i // 2) % n)


def peer(me, t):
    z, y, x = me // 16, (me // 4) % 4, me % 4
    dz = zigzag(t % 8, 8)
    dy = zigzag((t // 8 + t) % 4, 4)
    dx = zigzag((t // 32 + t // 2) % 4, 4)
    return ((z + dz) % 8) * 16 + ((y + dy) % 4) * 4 + (x + dx) % 4


def kernel(
    shift,
    tile_block,
    lesser,
    greater,
    coulomb,
    tf_hbm,
    ti_hbm,
    pol_out,
    scr_out,
    src,
    got,
    spec,
    mix,
    polar,
    near,
    near_got,
    tf,
    ti,
    weights,
    swap,
    load_sem,
    in_send,
    in_recv,
    pol_send,
    pol_recv,
    near_send,
    near_recv,
):
    me = lax.axis_index("energy")
    core = lax.axis_index("mom")
    loads = [
        pltpu.make_async_copy(lesser.at[0], src.at[0], load_sem.at[0]),
        pltpu.make_async_copy(greater.at[0], src.at[1], load_sem.at[1]),
        pltpu.make_async_copy(tf_hbm, tf, load_sem.at[2]),
        pltpu.make_async_copy(ti_hbm, ti, load_sem.at[3]),
    ]
    for load in loads:
        load.start()

    barrier = pltpu.get_barrier_semaphore()

    def greet(c, m):
        pl.semaphore_signal(barrier, inc=1, device_id=(c, m), device_id_type=MESH)

    greet(me, 1 - core)

    @pl.loop(1, CHIPS)
    def _(t):
        c = peer(me, t)
        greet(c, core)
        greet(c, 1 - core)

    prepare(coulomb, weights, swap)
    for load in loads:
        load.wait()
    pl.semaphore_wait(barrier, 2 * CHIPS - 1)

    def everyone(remote, local):
        local()
        remote(me, 1 - core)

        @pl.loop(1, CHIPS)
        def _(t):
            c = peer(me, t)
            remote(c, core)
            remote(c, 1 - core)

    def send_in(b):
        def ends(c, m):
            column = pl.multiple_of((c * 2 + m) * 2 * PART + b * PART, PART)
            return src.at[:, :, :, pl.ds(column, PART)], got.at[b, :, :, core, me]

        def remote(c, m):
            a, z = ends(c, m)
            pltpu.make_async_remote_copy(
                a, z, in_send.at[b], in_recv.at[b], device_id=(c, m), device_id_type=MESH
            ).start()

        def local():
            a, z = ends(me, core)
            pltpu.make_async_copy(a, z, in_recv.at[b]).start()

        everyone(remote, local)

    def send_pol(b):
        column = pl.multiple_of((me * 2 + core) * 2 * PART + b * PART, PART)

        def ends(c, m):
            return polar.at[b, m, :, c], pol_out.at[0, :, :, pl.ds(column, PART)]

        def remote(c, m):
            a, z = ends(c, m)
            pltpu.make_async_remote_copy(
                a, z, pol_send.at[b], pol_recv, device_id=(c, m), device_id_type=MESH
            ).start()

        def local():
            a, z = ends(me, core)
            pltpu.make_async_copy(a, z, pol_recv).start()

        everyone(remote, local)

    def send_near():
        def ends(c, m):
            return near.at[m, c], near_got.at[me // 32, me % 32, core]

        def remote(c, m):
            a, z = ends(c, m)
            pltpu.make_async_remote_copy(
                a, z, near_send, near_recv, device_id=(c, m), device_id_type=MESH
            ).start()

        def local():
            a, z = ends(me, core)
            pltpu.make_async_copy(a, z, near_recv).start()

        everyone(remote, local)

    def wait_all(ref, sem):
        pltpu.make_async_copy(ref, ref, sem).wait()

    sent = pl.ds(0, (2 * CHIPS - 1) * PART)
    for b in range(2):
        send_in(b)
    for b in range(2):
        wait_all(got.at[b], in_recv.at[b])
        forward(got, b, tf, spec)
        products(shift, spec, mix)
        backward(b, ti, mix, swap, polar, near)
        if b == 1:
            send_near()
        send_pol(b)
    wait_all(near_got, near_recv)
    screening(tile_block, weights, near_got, scr_out)
    wait_all(pol_out, pol_recv)
    for b in range(2):
        wait_all(src.at[:, :, :, sent], in_send.at[b])
        wait_all(src.at[0, :, :, sent], pol_send.at[b])
    wait_all(src.at[0, 0, :, sent], near_send)


def shards(lesser, greater, coulomb, tile_block, shift_table):
    tf, ti = tables()
    bf16, f32 = jnp.bfloat16, jnp.float32
    hbm = pl.BlockSpec(memory_space=pl.ANY)
    smem = pl.BlockSpec(memory_space=pltpu.SMEM)
    vmem = pl.BlockSpec(memory_space=pltpu.VMEM)
    polarization, screened = pl.pallas_call(
        kernel,
        out_shape=(
            jax.ShapeDtypeStruct((1, 2, E // CHIPS, NNZ), bf16),
            jax.ShapeDtypeStruct((2, 4, L, PART), f32),
        ),
        in_specs=[smem, smem, hbm, hbm, vmem, hbm, hbm],
        out_specs=(hbm, vmem),
        scratch_shapes=[
            pltpu.VMEM((2, 2, E // CHIPS, NNZ), bf16),
            pltpu.VMEM((2, 2, 2, 2, CHIPS, E // CHIPS, PART), bf16),
            pltpu.VMEM((2, 2, BLOCKS, 2, FREQ, PART), f32),
            pltpu.VMEM((2, 2, BLOCKS, 2, FREQ, PART), bf16),
            pltpu.VMEM((2, 2, 2, CHIPS, E // CHIPS, PART), bf16),
            pltpu.VMEM((2, L, 2, 2, PART), bf16),
            pltpu.VMEM((4, 32, 2, 2, 2, PART), bf16),
            pltpu.VMEM((2, 2 * FREQ, 2 * L), bf16),
            pltpu.VMEM((2, 2 * L, 2 * FREQ), bf16),
            pltpu.VMEM((2, 2 * L, 4 * L), bf16),
            pltpu.VMEM((2 * L, 2 * L), bf16),
            pltpu.SemaphoreType.DMA((4,)),
            pltpu.SemaphoreType.DMA((2,)),
            pltpu.SemaphoreType.DMA((2,)),
            pltpu.SemaphoreType.DMA((2,)),
            pltpu.SemaphoreType.DMA,
            pltpu.SemaphoreType.DMA,
            pltpu.SemaphoreType.DMA,
        ],
        compiler_params=pltpu.CompilerParams(
            collective_id=0, has_side_effects=True, vmem_limit_bytes=48 << 20
        ),
        name="polarization",
    )(shift_table, tile_block, lesser, greater, coulomb, jnp.asarray(tf), jnp.asarray(ti))
    return (polarization, screened.reshape(1, 2, 1, NNZ))


def solution(mesh):
    return jax.shard_map(
        shards,
        mesh=mesh,
        in_specs=(
            P("mom", None, "energy", None),
            P("mom", None, "energy", None),
            P("mom", None, None, None),
            P(),
            P(),
        ),
        out_specs=(P("mom", None, "energy", None), P("mom", None, "energy", None)),
        check_vma=False,
    )
```

time: 779 us -> 117 us (0.15); the launches traced: 768 us -> 117 us
  local copies, waits for them, and re-layouts: 541 us -> 8.53 us
  Pallas kernels: 0 us -> 108 us
  blocking collectives: 80.4 us -> 0 us
  waiting for transfers between devices: 47 us -> 0 us
  matrix products: 39.7 us -> 0 us
  other arithmetic: 21.5 us -> 0 us
  starting transfers between devices: 19.8 us -> 0 us
  between operations: 18 us -> 0.65 us
    unnamed x16, local copies, waits for them, and re-layouts: 378 us -> 8.53 us
    all_to_all x7 -> x0, local copies, waits for them, and re-layouts: 135 us -> none  [the longest x2 66.5 us: shards(): lax.all_to_all(greater, 'energy', split_axis=3, concat_axis=2, tiled=True)]
    pallas_call x0 -> x1, Pallas kernels: none -> 108 us  [shards(): pl.pallas_call(kernel, out_shape=(jax.ShapeDtypeStruct((1, 2, E // CHIPS,...]
    all_to_all x2 -> x0, blocking collectives: 80.4 us -> none  [the longest x1 44.7 us: shards(): lax.all_to_all(lesser, 'energy', split_axis=3, concat_axis=2, tiled=True)]
    dot_general x48 -> x0, matrix products: 39.7 us -> none  [the longest x40 38.4 us: complex_einsum(): jnp.einsum(form, table, data, precision=lax.Precision.HIGH, preferred_ele...]
    all_to_all x2 -> x0, waiting for transfers between devices: 37.6 us -> none  [the longest x1 23.8 us: shards(): lax.all_to_all(polar_cols, 'energy', split_axis=2, concat_axis=3, tiled=T...]
    all_to_all x2 -> x0, starting transfers between devices: 19.8 us -> none  [the longest x1 13.6 us: shards(): lax.all_to_all(polar_cols[:, :, :E // 4], 'energy', split_axis=2, concat_...]
    slice x38 -> x0, local copies, waits for them, and re-layouts: 17.5 us -> none  [the longest x8 9.2 us: spectrum(): pair[0].astype(jnp.float32)]
  transfers between devices with their start and end apart: 4 -> 0, of which waited for: 3 -> 0; matrix products, arithmetic and copies ran while one was open for 33% -> 0% of each run, Pallas kernels for 0% -> 0%
where the time goes in v1:
time: 117 us
  Pallas kernels  108 us (92%)
  local copies, waits for them, and re-layouts  8.53 us (7%)
    pallas_call x1, Pallas kernels, shards(): pl.pallas_call(kernel, out_shape=(jax.ShapeDtypeStruct((1, 2, E // CHIPS,...  108 us
    unnamed x16, local copies, waits for them, and re-layouts  8.53 us

profile of v1, /device:TPU:1, one launch (start us, length us, event | category | flops | bytes accessed | tf_op | source)
XLA Modules:
  0.0 116.9 jit_solution(8090101326651642583)
XLA Ops:
  0.6 0.0 copy-start
  0.6 1.2 %copy-done = bf16[1,2,4,65536]{3,2,1,0:T(4,128)(2,1)S(1)} copy-done((bf16[1,2,4,65536]{3,2,1,0:T(4,128)(2,1)S(1)}, bf16[1,2,4,65536]{3,2,1,0:T(4,128)(2,1)}, u32[]{:S(2)}) %copy-start) | copy-done | bytes 1048600
  1.9 0.0 copy-start.1
  1.9 1.2 %copy-done.1 = bf16[1,2,4,65536]{3,2,1,0:T(4,128)(2,1)S(1)} copy-done((bf16[1,2,4,65536]{3,2,1,0:T(4,128)(2,1)S(1)}, bf16[1,2,4,65536]{3,2,1,0:T(4,128)(2,1)}, u32[]{:S(2)}) %copy-start.1) | copy-done | bytes 1048600
  3.1 0.0 copy-start.2
  3.1 1.0 copy-done.2
  4.1 0.0 copy-start.3
  4.1 1.0 copy-done.3
  5.2 0.0 copy-start.4
  5.2 0.9 copy-done.4
  6.1 0.0 copy-start.5
  6.1 0.7 copy-done.5
  6.8 0.0 copy-start.6
  6.8 0.7 copy-done.6
  7.4 107.8 %polarization.1 = (bf16[1,2,4,65536]{3,2,1,0:T(4,128)(2,1)S(1)}, f32[2,4,128,128]{3,2,1,0:T(8,128)S(1)}) custom-call(s32[2,2]{1,0:T(2,128)S(1)} %copy-done.5, s32[4]{0:T(128)S(1)} %copy-done.6, bf16[1,2,4,65536]{3,2,1,0:T(4,128)(2,1)S(1)} %copy-done, bf16[1,2,4,65536]{3,2,1,0:T(4,128)(2,1)S(1)} %copy-done.1, bf16[1,4,128,128]{3,2,1,0:T(8,128)(2,1)S(1)} %copy-done.4, ...), custom_call_target="tpu_custom_call" | custom-call | tf_op jit(solution)/shard_map/polarization/pallas_call | solution.py:306
  115.2 1.0 copy.12
  116.1 0.8 copy.13
Async XLA Ops:
  0.6 1.2 %copy-start = (bf16[1,2,4,65536]{3,2,1,0:T(4,128)(2,1)S(1)}, bf16[1,2,4,65536]{3,2,1,0:T(4,128)(2,1)}, u32[]{:S(2)}) copy-start(bf16[1,2,4,65536]{3,2,1,0:T(4,128)(2,1)} %lesser.1) | copy-start | bytes 3145732
  1.9 1.2 %copy-start.1 = (bf16[1,2,4,65536]{3,2,1,0:T(4,128)(2,1)S(1)}, bf16[1,2,4,65536]{3,2,1,0:T(4,128)(2,1)}, u32[]{:S(2)}) copy-start(bf16[1,2,4,65536]{3,2,1,0:T(4,128)(2,1)} %greater.1) | copy-start | bytes 3145732
  3.1 1.0 copy-start.2
  4.1 1.0 copy-start.3
  5.2 0.9 copy-start.4
  6.1 0.7 copy-start.5
  6.8 0.7 copy-start.6

commit v2 on v1

--- a/solution.py
+++ b/solution.py
@@ -56,39 +56,38 @@
                 ]
 
 
-def products(shift, spec, mix):
-    for q in range(2):
-        for odd in range(2):
-
-            @pl.loop(0, L // 16)
-            def _(tile):
-                rows = pl.ds(pl.multiple_of(odd * L + tile * 16, 16), 16)
-                total = [[None, None] for _ in range(BLOCKS)]
-
-                def add(d, part, value):
-                    old = total[d][part]
-                    total[d][part] = value if old is None else old + value
-
-                for k in range(2):
-                    other = shift[q, k]
-                    left = [[spec[0, k, a, part, rows] for part in range(2)] for a in range(BLOCKS)]
-                    for c in range(BLOCKS):
-                        right_re = spec[1, other, c, 0, rows]
-                        right_im = spec[1, other, c, 1, rows]
-                        for d in range(BLOCKS - c):
-                            re, im = left[c + d]
-                            add(d, 0, re * right_re + im * right_im)
-                            add(d, 1, im * right_re - re * right_im)
-                for d in range(BLOCKS):
-                    for part in range(2):
-                        value = total[d][part]
-                        if d + 1 < BLOCKS:
-                            nxt = total[d + 1][part]
-                            value = value - nxt if odd else value + nxt
-                        high = value.astype(jnp.bfloat16)
-                        low = (value - high.astype(jnp.float32)).astype(jnp.bfloat16)
-                        mix[0, q, d, part, rows] = high
-                        mix[1, q, d, part, rows] = low
+def products(q, shift, spec, mix):
+    for odd in range(2):
+
+        @pl.loop(0, L // 16)
+        def _(tile):
+            rows = pl.ds(pl.multiple_of(odd * L + tile * 16, 16), 16)
+            total = [[None, None] for _ in range(BLOCKS)]
+
+            def add(d, part, value):
+                old = total[d][part]
+                total[d][part] = value if old is None else old + value
+
+            for k in range(2):
+                other = shift[q, k]
+                left = [[spec[0, k, a, part, rows] for part in range(2)] for a in range(BLOCKS)]
+                for c in range(BLOCKS):
+                    right_re = spec[1, other, c, 0, rows]
+                    right_im = spec[1, other, c, 1, rows]
+                    for d in range(BLOCKS - c):
+                        re, im = left[c + d]
+                        add(d, 0, re * right_re + im * right_im)
+                        add(d, 1, im * right_re - re * right_im)
+            for d in range(BLOCKS):
+                for part in range(2):
+                    value = total[d][part]
+                    if d + 1 < BLOCKS:
+                        nxt = total[d + 1][part]
+                        value = value - nxt if odd else value + nxt
+                    high = value.astype(jnp.bfloat16)
+                    low = (value - high.astype(jnp.float32)).astype(jnp.bfloat16)
+                    mix[0, q, d, part, rows] = high
+                    mix[1, q, d, part, rows] = low
 
 
 def backward(b, ti, mix, swap, polar, near):
@@ -143,16 +142,60 @@
                 ).astype(jnp.bfloat16)
 
 
-def zigzag(i, n):
-    return (i % 2) * ((i + 1) // 2) + (1 - i % 2) * ((n - i // 2) % n)
-
-
-def peer(me, t):
-    z, y, x = me // 16, (me // 4) % 4, me % 4
-    dz = zigzag(t % 8, 8)
-    dy = zigzag((t // 8 + t) % 4, 4)
-    dx = zigzag((t // 32 + t // 2) % 4, 4)
-    return ((z + dz) % 8) * 16 + ((y + dy) % 4) * 4 + (x + dx) % 4
+def place():
+    me = lax.axis_index("energy")
+    return lax.div(me, 16), lax.rem(lax.div(me, 4), 4), lax.rem(me, 4)
+
+
+def chip(z, y, x):
+    return z * 16 + y * 4 + x
+
+
+def greet_all(barrier, ready):
+    core = lax.axis_index("mom")
+    z, y, x = place()
+
+    def plane(sem):
+        @pl.loop(1, 16)
+        def _(t):
+            c = chip(z, lax.rem(y + lax.div(t, 4), 4), lax.rem(x + lax.rem(t, 4), 4))
+            pl.semaphore_signal(sem, inc=1, device_id=(c, core), device_id_type=MESH)
+
+    plane(barrier)
+    pl.semaphore_signal(barrier, inc=1, device_id=(chip(z, y, x), 1 - core), device_id_type=MESH)
+
+    @pl.loop(1, 8)
+    def _(t):
+        c = chip(lax.rem(z + t, 8), y, x)
+        for m in range(2):
+            pl.semaphore_signal(barrier, inc=1, device_id=(c, m), device_id_type=MESH)
+
+    pl.semaphore_wait(barrier, 30)
+    plane(ready)
+    pl.semaphore_wait(ready, 15)
+
+
+def peers(group, act):
+    core = lax.axis_index("mom")
+    z, y, x = place()
+    for i, dz in enumerate((0, 1, 7, 2, 6, 3, 5, 4)):
+        row = lax.rem(y + group + i, 4)
+        col = lax.rem(x + lax.div(jnp.int32(group), 4) + i // 2, 4)
+        c = chip(lax.rem(z + dz, 8), row, col)
+        if not (isinstance(group, int) and group == 0 and i == 0):
+            act(c, core)
+        act(c, 1 - core)
+
+
+def send(first, last, remote, local):
+    if first == 0:
+        local()
+        peers(0, remote)
+        first = 1
+
+    @pl.loop(first, last)
+    def _(group):
+        peers(group, remote)
 
 
 def kernel(
@@ -176,6 +219,7 @@
     ti,
     weights,
     swap,
+    ready,
     load_sem,
     in_send,
     in_recv,
@@ -196,34 +240,11 @@
         load.start()
 
     barrier = pltpu.get_barrier_semaphore()
-
-    def greet(c, m):
-        pl.semaphore_signal(barrier, inc=1, device_id=(c, m), device_id_type=MESH)
-
-    greet(me, 1 - core)
-
-    @pl.loop(1, CHIPS)
-    def _(t):
-        c = peer(me, t)
-        greet(c, core)
-        greet(c, 1 - core)
-
-    prepare(coulomb, weights, swap)
-    for load in loads:
+    greet_all(barrier, ready)
+    for load in loads[:2]:
         load.wait()
-    pl.semaphore_wait(barrier, 2 * CHIPS - 1)
-
-    def everyone(remote, local):
-        local()
-        remote(me, 1 - core)
-
-        @pl.loop(1, CHIPS)
-        def _(t):
-            c = peer(me, t)
-            remote(c, core)
-            remote(c, 1 - core)
-
-    def send_in(b):
+
+    def send_in(b, first, last):
         def ends(c, m):
             column = pl.multiple_of((c * 2 + m) * 2 * PART + b * PART, PART)
             return src.at[:, :, :, pl.ds(column, PART)], got.at[b, :, :, core, me]
@@ -238,9 +259,9 @@
             a, z = ends(me, core)
             pltpu.make_async_copy(a, z, in_recv.at[b]).start()
 
-        everyone(remote, local)
-
-    def send_pol(b):
+        send(first, last, remote, local)
+
+    def send_pol(b, first, last):
         column = pl.multiple_of((me * 2 + core) * 2 * PART + b * PART, PART)
 
         def ends(c, m):
@@ -256,7 +277,7 @@
             a, z = ends(me, core)
             pltpu.make_async_copy(a, z, pol_recv).start()
 
-        everyone(remote, local)
+        send(first, last, remote, local)
 
     def send_near():
         def ends(c, m):
@@ -272,22 +293,30 @@
             a, z = ends(me, core)
             pltpu.make_async_copy(a, z, near_recv).start()
 
-        everyone(remote, local)
+        send(0, 16, remote, local)
 
     def wait_all(ref, sem):
         pltpu.make_async_copy(ref, ref, sem).wait()
 
+    def compute(b):
+        forward(got, b, tf, spec)
+        for q in range(2):
+            products(q, shift, spec, mix)
+        backward(b, ti, mix, swap, polar, near)
+
     sent = pl.ds(0, (2 * CHIPS - 1) * PART)
-    for b in range(2):
-        send_in(b)
-    for b in range(2):
-        wait_all(got.at[b], in_recv.at[b])
-        forward(got, b, tf, spec)
-        products(shift, spec, mix)
-        backward(b, ti, mix, swap, polar, near)
-        if b == 1:
-            send_near()
-        send_pol(b)
+    send_in(0, 0, 16)
+    send_in(1, 0, 16)
+    prepare(coulomb, weights, swap)
+    for load in loads[2:]:
+        load.wait()
+    wait_all(got.at[0], in_recv.at[0])
+    compute(0)
+    send_pol(0, 0, 16)
+    wait_all(got.at[1], in_recv.at[1])
+    compute(1)
+    send_near()
+    send_pol(1, 0, 16)
     wait_all(near_got, near_recv)
     screening(tile_block, weights, near_got, scr_out)
     wait_all(pol_out, pol_recv)
@@ -303,6 +332,7 @@
     hbm = pl.BlockSpec(memory_space=pl.ANY)
     smem = pl.BlockSpec(memory_space=pltpu.SMEM)
     vmem = pl.BlockSpec(memory_space=pltpu.VMEM)
+    operands = (shift_table, tile_block, lesser, greater, coulomb, jnp.asarray(tf), jnp.asarray(ti))
     polarization, screened = pl.pallas_call(
         kernel,
         out_shape=(
@@ -323,6 +353,7 @@
             pltpu.VMEM((2, 2 * L, 2 * FREQ), bf16),
             pltpu.VMEM((2, 2 * L, 4 * L), bf16),
             pltpu.VMEM((2 * L, 2 * L), bf16),
+            pltpu.SemaphoreType.REGULAR,
             pltpu.SemaphoreType.DMA((4,)),
             pltpu.SemaphoreType.DMA((2,)),
             pltpu.SemaphoreType.DMA((2,)),
@@ -335,7 +366,7 @@
             collective_id=0, has_side_effects=True, vmem_limit_bytes=48 << 20
         ),
         name="polarization",
-    )(shift_table, tile_block, lesser, greater, coulomb, jnp.asarray(tf), jnp.asarray(ti))
+    )(*(pltpu.with_memory_space_constraint(operand, pltpu.HBM) for operand in operands))
     return (polarization, screened.reshape(1, 2, 1, NNZ))
 
 

time: 117 us -> 97.4 us (0.83)
  Pallas kernels: 108 us -> 94.9 us
  local copies, waits for them, and re-layouts: 8.53 us -> 1.77 us
    pallas_call x1, Pallas kernels: 108 us -> 94.9 us  [shards(): pl.pallas_call(kernel, out_shape=(jax.ShapeDtypeStruct((1, 2, E // CHIPS,...]
    unnamed x16 -> x2, local copies, waits for them, and re-layouts: 8.53 us -> 1.77 us
where the time goes in v2:
time: 97.4 us; the launch traced here: 97.3 us
  Pallas kernels  94.9 us (97%)
  local copies, waits for them, and re-layouts  1.77 us (2%)
    pallas_call x1, Pallas kernels, shards(): pl.pallas_call(kernel, out_shape=(jax.ShapeDtypeStruct((1, 2, E // CHIPS,...  94.9 us

profile of v2, /device:TPU:1, one launch (start us, length us, event | category | flops | bytes accessed | tf_op | source)
XLA Modules:
  0.0 97.3 jit_solution(13968797990364282874)
XLA Ops:
  0.6 94.9 %polarization.1 = (bf16[1,2,4,65536]{3,2,1,0:T(4,128)(2,1)S(1)}, f32[2,4,128,128]{3,2,1,0:T(8,128)S(1)}) custom-call(s32[2,2]{1,0:T(2,128)} %shift.1, s32[4]{0:T(128)} %tile_block.1, bf16[1,2,4,65536]{3,2,1,0:T(4,128)(2,1)} %lesser.1, bf16[1,2,4,65536]{3,2,1,0:T(4,128)(2,1)} %greater.1, bf16[1,4,128,128]{3,2,1,0:T(8,128)(2,1)} %coulomb.1, ...), custom_call_target="tpu_custom_call" | custom-call | tf_op jit(solution)/shard_map/polarization/pallas_call | solution.py:336
  95.5 1.0 copy.12
  96.5 0.8 copy.13

commit v3 on v2

--- a/solution.py
+++ b/solution.py
@@ -1,3 +1,4 @@
+import functools
 import math
 
 import jax
@@ -90,22 +91,21 @@
                     mix[1, q, d, part, rows] = low
 
 
-def backward(b, ti, mix, swap, polar, near):
-    for q in range(2):
-        for pair in range(2):
-            datas = []
-            for level in range(2):
-                halves = [mix[level, q, pair * 2 + h].reshape(2 * FREQ, PART) for h in range(2)]
-                datas.append(jnp.concatenate(halves, axis=1))
-            result = dot(ti[0], datas[0]) + dot(ti[0], datas[1]) + dot(ti[1], datas[0])
-            result = result.astype(jnp.bfloat16)
-            for h in range(2):
-                for s in range(2):
-                    value = result[s * L : (s + 1) * L, h * PART : (h + 1) * PART]
-                    polar[b, q, s, pl.ds((pair * 2 + h) * 32, 32)] = value.reshape(32, 4, PART)
-            if pair == 0:
-                value = dot(swap[...], result[:, :PART]).astype(jnp.bfloat16)
-                near[q, :, b] = value.reshape(L, 2, PART)
+def backward(q, b, ti, mix, swap, polar, near):
+    for pair in range(2):
+        datas = []
+        for level in range(2):
+            halves = [mix[level, q, pair * 2 + h].reshape(2 * FREQ, PART) for h in range(2)]
+            datas.append(jnp.concatenate(halves, axis=1))
+        result = dot(ti[0], datas[0]) + dot(ti[0], datas[1]) + dot(ti[1], datas[0])
+        result = result.astype(jnp.bfloat16)
+        for h in range(2):
+            for s in range(2):
+                value = result[s * L : (s + 1) * L, h * PART : (h + 1) * PART]
+                polar[b, q, s, pl.ds((pair * 2 + h) * 32, 32)] = value.reshape(32, 4, PART)
+        if pair == 0:
+            value = dot(swap[...], result[:, :PART]).astype(jnp.bfloat16)
+            near[q, :, b] = value.reshape(L, 2, PART)
 
 
 def screening(tile_block, weights, got, out):
@@ -151,7 +151,7 @@
     return z * 16 + y * 4 + x
 
 
-def greet_all(barrier, ready):
+def greet(barrier, ready):
     core = lax.axis_index("mom")
     z, y, x = place()
 
@@ -172,30 +172,63 @@
 
     pl.semaphore_wait(barrier, 30)
     plane(ready)
-    pl.semaphore_wait(ready, 15)
-
-
-def peers(group, act):
+
+
+STEPS = (0, 1, 7, 2, 6, 3, 5, 4)
+
+
+def line(act):
     core = lax.axis_index("mom")
     z, y, x = place()
-    for i, dz in enumerate((0, 1, 7, 2, 6, 3, 5, 4)):
-        row = lax.rem(y + group + i, 4)
-        col = lax.rem(x + lax.div(jnp.int32(group), 4) + i // 2, 4)
-        c = chip(lax.rem(z + dz, 8), row, col)
-        if not (isinstance(group, int) and group == 0 and i == 0):
-            act(c, core)
+    act(chip(z, y, x), 1 - core)
+    for dz in STEPS[1:]:
+        c = chip(lax.rem(z + dz, 8), y, x)
+        act(c, core)
         act(c, 1 - core)
 
 
-def send(first, last, remote, local):
-    if first == 0:
+def others(act):
+    z, y, x = place()
+
+    @pl.loop(0, 16)
+    def _(group):
+        for i, dz in enumerate(STEPS):
+            own = (-(i // 2)) % 4 * 4 + (-i) % 4
+
+            @pl.when(group != own)
+            def _():
+                row = lax.rem(y + group + i, 4)
+                col = lax.rem(x + lax.div(group, 4) + i // 2, 4)
+                act(chip(lax.rem(z + dz, 8), row, col))
+
+
+def both_cores(remote, core, c):
+    remote(c, core)
+    remote(c, 1 - core)
+
+
+def send(remote, local):
+    core = lax.axis_index("mom")
+    local()
+    line(remote)
+    others(functools.partial(both_cores, remote, core))
+
+
+def send_to(q, remote, local):
+    core = lax.axis_index("mom")
+    z, y, x = place()
+
+    @pl.when(core == q)
+    def _():
         local()
-        peers(0, remote)
-        first = 1
-
-    @pl.loop(first, last)
-    def _(group):
-        peers(group, remote)
+
+    @pl.when(core != q)
+    def _():
+        remote(chip(z, y, x), q)
+
+    for dz in STEPS[1:]:
+        remote(chip(lax.rem(z + dz, 8), y, x), q)
+    others(lambda c: remote(c, q))
 
 
 def kernel(
@@ -240,83 +273,67 @@
         load.start()
 
     barrier = pltpu.get_barrier_semaphore()
-    greet_all(barrier, ready)
+    greet(barrier, ready)
     for load in loads[:2]:
         load.wait()
 
-    def send_in(b, first, last):
-        def ends(c, m):
+    def copies(source, target, send_sem, recv_sem):
+        def remote(c, m):
+            pltpu.make_async_remote_copy(
+                source(c, m), target, send_sem, recv_sem, device_id=(c, m), device_id_type=MESH
+            ).start()
+
+        def local():
+            pltpu.make_async_copy(source(me, core), target, recv_sem).start()
+
+        return remote, local
+
+    def copies_in(b):
+        def source(c, m):
             column = pl.multiple_of((c * 2 + m) * 2 * PART + b * PART, PART)
-            return src.at[:, :, :, pl.ds(column, PART)], got.at[b, :, :, core, me]
-
-        def remote(c, m):
-            a, z = ends(c, m)
-            pltpu.make_async_remote_copy(
-                a, z, in_send.at[b], in_recv.at[b], device_id=(c, m), device_id_type=MESH
-            ).start()
-
-        def local():
-            a, z = ends(me, core)
-            pltpu.make_async_copy(a, z, in_recv.at[b]).start()
-
-        send(first, last, remote, local)
-
-    def send_pol(b, first, last):
+            return src.at[:, :, :, pl.ds(column, PART)]
+
+        return copies(source, got.at[b, :, :, core, me], in_send.at[b], in_recv.at[b])
+
+    def copies_pol(b):
         column = pl.multiple_of((me * 2 + core) * 2 * PART + b * PART, PART)
-
-        def ends(c, m):
-            return polar.at[b, m, :, c], pol_out.at[0, :, :, pl.ds(column, PART)]
-
-        def remote(c, m):
-            a, z = ends(c, m)
-            pltpu.make_async_remote_copy(
-                a, z, pol_send.at[b], pol_recv, device_id=(c, m), device_id_type=MESH
-            ).start()
-
-        def local():
-            a, z = ends(me, core)
-            pltpu.make_async_copy(a, z, pol_recv).start()
-
-        send(first, last, remote, local)
-
-    def send_near():
-        def ends(c, m):
-            return near.at[m, c], near_got.at[me // 32, me % 32, core]
-
-        def remote(c, m):
-            a, z = ends(c, m)
-            pltpu.make_async_remote_copy(
-                a, z, near_send, near_recv, device_id=(c, m), device_id_type=MESH
-            ).start()
-
-        def local():
-            a, z = ends(me, core)
-            pltpu.make_async_copy(a, z, near_recv).start()
-
-        send(0, 16, remote, local)
+        return copies(
+            lambda c, m: polar.at[b, m, :, c],
+            pol_out.at[0, :, :, pl.ds(column, PART)],
+            pol_send.at[b],
+            pol_recv,
+        )
+
+    def copies_near():
+        place_of = near_got.at[lax.div(me, 32), lax.rem(me, 32), core]
+        return copies(lambda c, m: near.at[m, c], place_of, near_send, near_recv)
 
     def wait_all(ref, sem):
         pltpu.make_async_copy(ref, ref, sem).wait()
 
-    def compute(b):
+    sent = pl.ds(0, (2 * CHIPS - 1) * PART)
+    for b in range(2):
+        remote, local = copies_in(b)
+        line(remote)
+        local()
+    pl.semaphore_wait(ready, 15)
+    for b in range(2):
+        remote, _ = copies_in(b)
+        others(functools.partial(both_cores, remote, core))
+    prepare(coulomb, weights, swap)
+    for load in loads[2:]:
+        load.wait()
+    for b in range(2):
+        wait_all(got.at[b], in_recv.at[b])
         forward(got, b, tf, spec)
         for q in range(2):
             products(q, shift, spec, mix)
-        backward(b, ti, mix, swap, polar, near)
-
-    sent = pl.ds(0, (2 * CHIPS - 1) * PART)
-    send_in(0, 0, 16)
-    send_in(1, 0, 16)
-    prepare(coulomb, weights, swap)
-    for load in loads[2:]:
-        load.wait()
-    wait_all(got.at[0], in_recv.at[0])
-    compute(0)
-    send_pol(0, 0, 16)
-    wait_all(got.at[1], in_recv.at[1])
-    compute(1)
-    send_near()
-    send_pol(1, 0, 16)
+            backward(q, b, ti, mix, swap, polar, near)
+            if b == 1:
+                send_to(q, *copies_near())
+                send_to(q, *copies_pol(b))
+        if b == 0:
+            send(*copies_pol(b))
     wait_all(near_got, near_recv)
     screening(tile_block, weights, near_got, scr_out)
     wait_all(pol_out, pol_recv)

time: 97.4 us -> 93.9 us (0.964)
  Pallas kernels: 94.9 us -> 91.4 us
    pallas_call x1, Pallas kernels: 94.9 us -> 91.4 us  [shards(): pl.pallas_call(kernel, out_shape=(jax.ShapeDtypeStruct((1, 2, E // CHIPS,...]
where the time goes in v3:
time: 93.9 us; the launch traced here: 93.8 us
  Pallas kernels  91.4 us (97%)
  local copies, waits for them, and re-layouts  1.77 us (2%)
    pallas_call x1, Pallas kernels, shards(): pl.pallas_call(kernel, out_shape=(jax.ShapeDtypeStruct((1, 2, E // CHIPS,...  91.4 us

profile of v3, /device:TPU:1, one launch (start us, length us, event | category | flops | bytes accessed | tf_op | source)
XLA Modules:
  0.0 93.8 jit_solution(5777188815192903415)
XLA Ops:
  0.6 91.4 %polarization.1 = (bf16[1,2,4,65536]{3,2,1,0:T(4,128)(2,1)S(1)}, f32[2,4,128,128]{3,2,1,0:T(8,128)S(1)}) custom-call(s32[2,2]{1,0:T(2,128)} %shift.1, s32[4]{0:T(128)} %tile_block.1, bf16[1,2,4,65536]{3,2,1,0:T(4,128)(2,1)} %lesser.1, bf16[1,2,4,65536]{3,2,1,0:T(4,128)(2,1)} %greater.1, bf16[1,4,128,128]{3,2,1,0:T(8,128)(2,1)} %coulomb.1, ...), custom_call_target="tpu_custom_call" | custom-call | tf_op jit(solution)/shard_map/polarization/pallas_call | solution.py:353
  92.0 1.0 %copy.12 = bf16[1,2,4,65536]{3,2,1,0:T(4,128)(2,1)} copy(bf16[1,2,4,65536]{3,2,1,0:T(4,128)(2,1)S(1)} %get-tuple-element.10) | data formatting | bytes 2097152
  93.0 0.8 copy.13

commit v4 on v3

--- a/solution.py
+++ b/solution.py
@@ -174,7 +174,7 @@
     plane(ready)
 
 
-STEPS = (0, 1, 7, 2, 6, 3, 5, 4)
+STEPS = (0, 4, 3, 5, 2, 6, 1, 7)
 
 
 def line(act):

time: 93.9 us -> 91.7 us (0.977)
  Pallas kernels: 91.4 us -> 89.2 us
    pallas_call x1, Pallas kernels: 91.4 us -> 89.2 us  [shards(): pl.pallas_call(kernel, out_shape=(jax.ShapeDtypeStruct((1, 2, E // CHIPS,...]
where the time goes in v4:
time: 91.7 us; the launch traced here: 91.6 us
  Pallas kernels  89.2 us (97%)
  local copies, waits for them, and re-layouts  1.77 us (2%)
    pallas_call x1, Pallas kernels, shards(): pl.pallas_call(kernel, out_shape=(jax.ShapeDtypeStruct((1, 2, E // CHIPS,...  89.2 us

profile of v4, /device:TPU:1, one launch (start us, length us, event | category | flops | bytes accessed | tf_op | source)
XLA Modules:
  0.0 91.6 jit_solution(533469739903970587)
XLA Ops:
  0.6 89.2 %polarization.1 = (bf16[1,2,4,65536]{3,2,1,0:T(4,128)(2,1)S(1)}, f32[2,4,128,128]{3,2,1,0:T(8,128)S(1)}) custom-call(s32[2,2]{1,0:T(2,128)} %shift.1, s32[4]{0:T(128)} %tile_block.1, bf16[1,2,4,65536]{3,2,1,0:T(4,128)(2,1)} %lesser.1, bf16[1,2,4,65536]{3,2,1,0:T(4,128)(2,1)} %greater.1, bf16[1,4,128,128]{3,2,1,0:T(8,128)(2,1)} %coulomb.1, ...), custom_call_target="tpu_custom_call" | custom-call | tf_op jit(solution)/shard_map/polarization/pallas_call | solution.py:353
  89.9 1.0 %copy.12 = bf16[1,2,4,65536]{3,2,1,0:T(4,128)(2,1)} copy(bf16[1,2,4,65536]{3,2,1,0:T(4,128)(2,1)S(1)} %get-tuple-element.10) | data formatting | bytes 2097152
  90.8 0.8 copy.13

commit v5 on v4

--- a/solution.py
+++ b/solution.py
@@ -151,7 +151,7 @@
     return z * 16 + y * 4 + x
 
 
-def greet(barrier, ready):
+def greet(barrier, ready, loads):
     core = lax.axis_index("mom")
     z, y, x = place()
 
@@ -170,8 +170,12 @@
         for m in range(2):
             pl.semaphore_signal(barrier, inc=1, device_id=(c, m), device_id_type=MESH)
 
+    for load in loads:
+        load.start()
     pl.semaphore_wait(barrier, 30)
     plane(ready)
+    for load in loads:
+        load.wait()
 
 
 STEPS = (0, 4, 3, 5, 2, 6, 1, 7)
@@ -232,15 +236,19 @@
 
 
 def kernel(
-    shift,
-    tile_block,
+    shift_hbm,
+    tile_hbm,
     lesser,
     greater,
-    coulomb,
+    coulomb_hbm,
     tf_hbm,
     ti_hbm,
     pol_out,
     scr_out,
+    shift,
+    tile_block,
+    coulomb,
+    screened,
     src,
     got,
     spec,
@@ -268,14 +276,13 @@
         pltpu.make_async_copy(greater.at[0], src.at[1], load_sem.at[1]),
         pltpu.make_async_copy(tf_hbm, tf, load_sem.at[2]),
         pltpu.make_async_copy(ti_hbm, ti, load_sem.at[3]),
+        pltpu.make_async_copy(shift_hbm, shift, load_sem.at[4]),
+        pltpu.make_async_copy(tile_hbm, tile_block, load_sem.at[5]),
+        pltpu.make_async_copy(coulomb_hbm, coulomb, load_sem.at[6]),
     ]
-    for load in loads:
+    greet(pltpu.get_barrier_semaphore(), ready, loads[:2])
+    for load in loads[2:]:
         load.start()
-
-    barrier = pltpu.get_barrier_semaphore()
-    greet(barrier, ready)
-    for load in loads[:2]:
-        load.wait()
 
     def copies(source, target, send_sem, recv_sem):
         def remote(c, m):
@@ -320,9 +327,9 @@
     for b in range(2):
         remote, _ = copies_in(b)
         others(functools.partial(both_cores, remote, core))
-    prepare(coulomb, weights, swap)
     for load in loads[2:]:
         load.wait()
+    prepare(coulomb, weights, swap)
     for b in range(2):
         wait_all(got.at[b], in_recv.at[b])
         forward(got, b, tf, spec)
@@ -335,8 +342,11 @@
         if b == 0:
             send(*copies_pol(b))
     wait_all(near_got, near_recv)
-    screening(tile_block, weights, near_got, scr_out)
+    screening(tile_block, weights, near_got, screened)
+    store = pltpu.make_async_copy(screened, scr_out, load_sem.at[7])
+    store.start()
     wait_all(pol_out, pol_recv)
+    store.wait()
     for b in range(2):
         wait_all(src.at[:, :, :, sent], in_send.at[b])
         wait_all(src.at[0, :, :, sent], pol_send.at[b])
@@ -347,8 +357,6 @@
     tf, ti = tables()
     bf16, f32 = jnp.bfloat16, jnp.float32
     hbm = pl.BlockSpec(memory_space=pl.ANY)
-    smem = pl.BlockSpec(memory_space=pltpu.SMEM)
-    vmem = pl.BlockSpec(memory_space=pltpu.VMEM)
     operands = (shift_table, tile_block, lesser, greater, coulomb, jnp.asarray(tf), jnp.asarray(ti))
     polarization, screened = pl.pallas_call(
         kernel,
@@ -356,9 +364,13 @@
             jax.ShapeDtypeStruct((1, 2, E // CHIPS, NNZ), bf16),
             jax.ShapeDtypeStruct((2, 4, L, PART), f32),
         ),
-        in_specs=[smem, smem, hbm, hbm, vmem, hbm, hbm],
-        out_specs=(hbm, vmem),
+        in_specs=[hbm] * 7,
+        out_specs=(hbm, hbm),
         scratch_shapes=[
+            pltpu.SMEM((2, 2), jnp.int32),
+            pltpu.SMEM((4,), jnp.int32),
+            pltpu.VMEM((1, 4, L, PART), bf16),
+            pltpu.VMEM((2, 4, L, PART), f32),
             pltpu.VMEM((2, 2, E // CHIPS, NNZ), bf16),
             pltpu.VMEM((2, 2, 2, 2, CHIPS, E // CHIPS, PART), bf16),
             pltpu.VMEM((2, 2, BLOCKS, 2, FREQ, PART), f32),
@@ -371,7 +383,7 @@
             pltpu.VMEM((2, 2 * L, 4 * L), bf16),
             pltpu.VMEM((2 * L, 2 * L), bf16),
             pltpu.SemaphoreType.REGULAR,
-            pltpu.SemaphoreType.DMA((4,)),
+            pltpu.SemaphoreType.DMA((8,)),
             pltpu.SemaphoreType.DMA((2,)),
             pltpu.SemaphoreType.DMA((2,)),
             pltpu.SemaphoreType.DMA((2,)),

time: 91.7 us -> 90.8 us (level)
  no operation moved by 1% of the time
where the time goes in v5:
time: 90.8 us; the launch traced here: 90.7 us
  Pallas kernels  88.3 us (97%)
  local copies, waits for them, and re-layouts  1.77 us (2%)
    pallas_call x1, Pallas kernels, shards(): pl.pallas_call(kernel, out_shape=(jax.ShapeDtypeStruct((1, 2, E // CHIPS,...  88.3 us

profile of v5, /device:TPU:1, one launch (start us, length us, event | category | flops | bytes accessed | tf_op | source)
XLA Modules:
  0.0 90.7 jit_solution(7219715169089397591)
XLA Ops:
  0.6 88.3 %polarization.1 = (bf16[1,2,4,65536]{3,2,1,0:T(4,128)(2,1)S(1)}, f32[2,4,128,128]{3,2,1,0:T(8,128)S(1)}) custom-call(s32[2,2]{1,0:T(2,128)} %shift_hbm.1, s32[4]{0:T(128)} %tile_hbm.1, bf16[1,2,4,65536]{3,2,1,0:T(4,128)(2,1)} %lesser.1, bf16[1,2,4,65536]{3,2,1,0:T(4,128)(2,1)} %greater.1, bf16[1,4,128,128]{3,2,1,0:T(8,128)(2,1)} %coulomb_hbm.1, ...), custom_call_target="tpu_custom_call" | custom-call | tf_op jit(solution)/shard_map/polarization/pallas_call | solution.py:361
  89.0 1.0 %copy.12 = bf16[1,2,4,65536]{3,2,1,0:T(4,128)(2,1)} copy(bf16[1,2,4,65536]{3,2,1,0:T(4,128)(2,1)S(1)} %get-tuple-element.10) | data formatting | bytes 2097152
  89.9 0.8 copy.13
